TPU v7x, 128 devices: a whole 4x4x4 slice. The times are simulated.
128 devices in a mesh: fsdp: 64 (over x, y, z_lo, core), tp: 2 (over z_hi).
Axes of the slice: x: 4, y: 4, z: 4 (z_hi: 2, z_lo: 2; z = z_hi * 2 + z_lo), core: 2. Of those that a mesh axis runs over, the one named last changes fastest.
Arguments:
- inputs: float32 [25600, 768], P(('fsdp', 'tp')), may hold values from -6 to 6
- routes: int32 [25600, 2], P('fsdp'), may hold values from 0 to 15, all different within a row; in each aligned block of 400 rows (0 to 399, 400 to 799, ...) at most 63 rows name the same one
- attention_norm_gain: bfloat16 [768], P('fsdp'), may hold values from 0.099609375 to 1.8984375
- attention_norm_shift: bfloat16 [768], P('fsdp'), may hold values from -3 to 3
- qkv_weight: bfloat16 [3, 768, 768], P(None, 'fsdp', 'tp'), may hold values from -0.21875 to 0.21875
- proj_weight: bfloat16 [768, 768], P('tp', 'fsdp'), may hold values from -0.875 to 0.875
- expert_norm_gain: bfloat16 [768], P('fsdp'), may hold values from 0.099609375 to 1.8984375
- expert_norm_shift: bfloat16 [768], P('fsdp'), may hold values from -3 to 3
- router_weight: bfloat16 [768, 16], P('fsdp'), may hold values from -0.109375 to 0.109375
- expert_in: bfloat16 [768, 16, 3072], P('fsdp', None, 'tp'), may hold values from -0.21875 to 0.21875
- expert_out: bfloat16 [768, 16, 3072], P('fsdp', None, 'tp'), may hold values from -0.4375 to 0.4375
- cotangent: float32 [25600, 768], P(('fsdp', 'tp')), may hold values from -6 to 6
Outputs:
- outputs: float32 [25600, 768], P(('fsdp', 'tp'))
- input_grad: float32 [25600, 768], P(('fsdp', 'tp'))
- attn_gain_grad: float32 [768], P('fsdp')
- attn_shift_grad: float32 [768], P('fsdp')
- qkv_grad: float32 [3, 768, 768], P(None, 'fsdp', 'tp')
- proj_grad: float32 [768, 768], P('tp', 'fsdp')
- moe_gain_grad: float32 [768], P('fsdp')
- moe_shift_grad: float32 [768], P('fsdp')
- router_grad: float32 [768, 16], P('fsdp')
- expert_in_grad: float32 [768, 16, 3072], P('fsdp', None, 'tp')
- expert_out_grad: float32 [768, 16, 3072], P('fsdp', None, 'tp')
Inputs may be any that keep to these rules, and one draw needn't show every extreme that they name: `routes`: in each aligned block of 400 rows (one routing group) the two experts of a row differ and no expert is named by more than 63 rows; some expert is named by exactly 63 rows of some block.
All inputs are finite; a program needn't handle non-finite values.
Results may differ from a plain program's by a relative error of at most 0.01.
Values may be sent and summed in bfloat16 or wider, within the bound.
A program may use at most 192 MiB of HBM per device.

v0:
```python
import jax
import jax.numpy as jnp
from jax import lax
from jax.sharding import PartitionSpec as P

HEAD_DIM = 64
SEQ = 200
REAL_TOK = 197
CAP = 63
EPS = 1e-06
TOP = lax.Precision.HIGHEST


def gelu_exact(value):
    return jax.nn.gelu(value, approximate=False)


def normalize_rows(value, norm_gain, norm_shift):
    row_mean = jnp.mean(value, axis=-1, keepdims=True)
    centered_rows = value - row_mean
    inverse_deviation = lax.rsqrt(
        jnp.mean(centered_rows * centered_rows, axis=-1, keepdims=True) + EPS
    )
    standardized_rows = centered_rows * inverse_deviation
    normed_rows = (
        standardized_rows * norm_gain.astype(jnp.float32) + norm_shift.astype(jnp.float32)
    ).astype(jnp.bfloat16)
    return (normed_rows, standardized_rows, inverse_deviation)


def norm_backward(incoming_gradient, standardized_rows, inverse_deviation, norm_gain):
    scaled_gradient = incoming_gradient * norm_gain.astype(jnp.float32)
    inner_product = (
        scaled_gradient
        - jnp.mean(scaled_gradient, axis=-1, keepdims=True)
        - standardized_rows * jnp.mean(scaled_gradient * standardized_rows, axis=-1, keepdims=True)
    )
    return (
        inverse_deviation * inner_product,
        jnp.sum(incoming_gradient * standardized_rows, axis=0),
        jnp.sum(incoming_gradient, axis=0),
    )


def slot_table(routes, experts, capacity):
    picked = (routes[:, :, None] == jnp.arange(experts, dtype=jnp.int32)[None, None, :]).astype(
        jnp.int32
    )
    flat = picked.reshape(-1, experts)
    before = jnp.cumsum(flat, axis=0) - flat
    number = jnp.sum(before * flat, axis=-1)
    slot = routes.reshape(-1) * capacity + number
    owner = jnp.arange(flat.shape[0], dtype=jnp.int32) // 2
    token_of_slot = jnp.zeros((experts * capacity,), jnp.int32).at[slot].set(owner)
    filled = jnp.zeros((experts * capacity,), jnp.int32).at[slot].set(1)
    return (picked, slot, token_of_slot, filled)


def split_heads(value, images):
    input_rows, width = value.shape
    return value.reshape(images, input_rows // images, width // HEAD_DIM, HEAD_DIM)


def live_keys(length):
    return (jnp.arange(length) < REAL_TOK)[None, None, None, :]


def attend(query, key, value, images):
    query_h = split_heads(query, images)
    key_h = split_heads(key, images)
    value_h = split_heads(value, images)
    scores = jnp.einsum(
        "ishd,ithd->ihst", query_h, key_h, preferred_element_type=jnp.float32
    ) * HEAD_DIM ** (-0.5)
    live = live_keys(scores.shape[-1])
    lse = jnp.log(jnp.sum(jnp.where(live, jnp.exp(scores), 0.0), axis=-1, keepdims=True))
    probs = jnp.where(live, jnp.exp(scores - lse), 0.0).astype(jnp.bfloat16)
    context = jnp.einsum(
        "ihst,ithd->ishd", probs, value_h, preferred_element_type=jnp.float32
    ).astype(jnp.bfloat16)
    return (context.reshape(query.shape), lse)


def attend_back(query, key, value, lse, context_grad, images):
    query_h = split_heads(query, images)
    key_h = split_heads(key, images)
    value_h = split_heads(value, images)
    grad_h = split_heads(context_grad, images)
    scores = jnp.einsum(
        "ishd,ithd->ihst", query_h, key_h, preferred_element_type=jnp.float32
    ) * HEAD_DIM ** (-0.5)
    live = live_keys(scores.shape[-1])
    probs = jnp.where(live, jnp.exp(scores - lse), 0.0)
    value_grad = jnp.einsum(
        "ihst,ishd->ithd", probs.astype(jnp.bfloat16), grad_h, preferred_element_type=jnp.float32
    ).astype(jnp.bfloat16)
    inner_product = jnp.einsum(
        "ishd,ithd->ihst", grad_h, value_h, preferred_element_type=jnp.float32
    )
    score_grad = (
        probs
        * (inner_product - jnp.sum(probs * inner_product, axis=-1, keepdims=True))
        * HEAD_DIM ** (-0.5)
    ).astype(jnp.bfloat16)
    query_grad = jnp.einsum(
        "ihst,ithd->ishd", score_grad, key_h, preferred_element_type=jnp.float32
    ).astype(jnp.bfloat16)
    key_grad = jnp.einsum(
        "ihst,ishd->ithd", score_grad, query_h, preferred_element_type=jnp.float32
    ).astype(jnp.bfloat16)
    shape = query.shape
    return (query_grad.reshape(shape), key_grad.reshape(shape), value_grad.reshape(shape))


def gather_dense(
    qkv_weight,
    proj_weight,
    router_weight,
    attention_norm_gain,
    attention_norm_shift,
    expert_norm_gain,
    expert_norm_shift,
):
    rows = qkv_weight.shape[1]
    heads_width = qkv_weight.shape[2]
    experts = router_weight.shape[1]
    packed = jnp.concatenate(
        [
            jnp.transpose(qkv_weight, (1, 0, 2)).reshape(rows, -1),
            proj_weight.T,
            router_weight,
            jnp.stack(
                [attention_norm_gain, attention_norm_shift, expert_norm_gain, expert_norm_shift],
                axis=1,
            ),
        ],
        axis=1,
    )
    full = lax.all_gather(packed, "fsdp", axis=0, tiled=True)
    width = full.shape[0]
    at = 3 * heads_width
    qkv_full = jnp.transpose(full[:, :at].reshape(width, 3, heads_width), (1, 0, 2))
    proj_full = full[:, at : at + heads_width].T
    at += heads_width
    router_full = full[:, at : at + experts]
    at += experts
    norms = full[:, at : at + 4]
    return (qkv_full, proj_full, router_full, norms[:, 0], norms[:, 1], norms[:, 2], norms[:, 3])


def reduce_dense(qkv_part, proj_part, router_part, norm_parts):
    width = qkv_part.shape[1]
    heads_width = qkv_part.shape[2]
    experts = router_part.shape[1]
    packed = jnp.concatenate(
        [
            jnp.transpose(qkv_part, (1, 0, 2)).reshape(width, -1),
            proj_part.T,
            router_part,
            jnp.stack(norm_parts, axis=1),
        ],
        axis=1,
    )
    part = lax.psum_scatter(packed, "fsdp", scatter_dimension=0, tiled=True)
    rows = part.shape[0]
    at = 3 * heads_width
    qkv_grad = jnp.transpose(part[:, :at].reshape(rows, 3, heads_width), (1, 0, 2))
    proj_grad = part[:, at : at + heads_width].T
    at += heads_width
    shared = lax.psum(part[:, at:], "tp")
    router_grad = shared[:, :experts]
    norm_grads = [shared[:, experts + i] for i in range(len(norm_parts))]
    return (qkv_grad, proj_grad, router_grad, norm_grads)


def group_rows(value):
    return lax.all_gather(value, "tp", axis=0, tiled=True)


def owned_rows(value):
    return lax.psum_scatter(value, "tp", scatter_dimension=0, tiled=True)


def to_owners(slots, holders):
    experts, capacity, width = slots.shape
    spread = jnp.broadcast_to(slots[:, None], (experts, holders, capacity, width)).reshape(
        experts * holders, capacity, width
    )
    moved = lax.all_to_all(spread, "fsdp", split_axis=0, concat_axis=0, tiled=True)
    return moved.reshape(-1, width)


def to_groups(partial_value, experts, holders, capacity):
    width = partial_value.shape[1]
    pieces = partial_value.reshape(experts * holders, capacity, width)
    moved = lax.all_to_all(pieces, "fsdp", split_axis=0, concat_axis=0, tiled=True)
    return jnp.sum(moved.reshape(experts, holders, capacity, width), axis=1)


def per_device(
    inputs,
    routes,
    attention_norm_gain,
    attention_norm_shift,
    qkv_weight,
    proj_weight,
    expert_norm_gain,
    expert_norm_shift,
    router_weight,
    expert_in,
    expert_out,
    cotangent,
):
    f32 = jnp.float32
    bf16 = jnp.bfloat16
    dense = gather_dense(
        qkv_weight,
        proj_weight,
        router_weight,
        attention_norm_gain,
        attention_norm_shift,
        expert_norm_gain,
        expert_norm_shift,
    )
    qkv_full, proj_full, router_full, attention_gain, attention_shift, expert_gain, expert_shift = (
        dense
    )
    group = routes.shape[0]
    images = group // SEQ
    experts = router_full.shape[1]
    width = qkv_full.shape[1]
    units = expert_in.shape[2]
    local_rows = expert_in.shape[0]
    holders = lax.axis_size("fsdp") // experts
    block_units = units // holders
    attention_normed, attention_standardized, attention_inverse_deviation = normalize_rows(
        inputs, attention_gain, attention_shift
    )
    tokens_a = group_rows(attention_normed)
    proj = jnp.einsum("td,idh->ith", tokens_a, qkv_full, preferred_element_type=f32).astype(bf16)
    context, lse = attend(proj[0], proj[1], proj[2], images)
    residual_middle = inputs + owned_rows(jnp.dot(context, proj_full, preferred_element_type=f32))
    expert_normed, expert_standardized, expert_inverse_deviation = normalize_rows(
        residual_middle, expert_gain, expert_shift
    )
    tokens_m = group_rows(expert_normed)
    logits = jnp.dot(tokens_m, router_full, preferred_element_type=f32)
    raised = jnp.exp(logits)
    probs = raised / jnp.sum(raised, axis=-1, keepdims=True)
    picked, slot, token_of_slot, filled = slot_table(routes, experts, CAP)
    gates = jnp.sum(picked.astype(f32) * probs[:, None, :], axis=-1)
    slotted = jnp.where(filled[:, None] > 0, tokens_m[token_of_slot], jnp.zeros((), bf16)).reshape(
        experts, CAP, width
    )
    regroup_in = expert_in.reshape(local_rows, experts * holders, block_units)
    regroup_out = expert_out.reshape(local_rows, experts * holders, block_units)
    own_in, own_out = (
        lax.all_to_all(regroup_in, "fsdp", split_axis=1, concat_axis=0, tiled=True),
        lax.all_to_all(regroup_out, "fsdp", split_axis=1, concat_axis=0, tiled=True),
    )
    own_in = own_in.reshape(width, block_units)
    own_out = own_out.reshape(width, block_units)
    owner_x = to_owners(slotted, holders)
    owner_pre = jnp.dot(owner_x, own_in, preferred_element_type=f32)
    owner_hidden = gelu_exact(owner_pre).astype(bf16)
    owner_res = jnp.einsum("cf,df->cd", owner_hidden, own_out, preferred_element_type=f32)
    expert_res = to_groups(owner_res, experts, holders, CAP)
    routed = expert_res.reshape(experts * CAP, width)[slot].reshape(group, 2, width)
    outputs = residual_middle + owned_rows(jnp.sum(gates[:, :, None] * routed, axis=1))
    qkv_back, proj_back, router_back = (qkv_full, proj_full, router_full)
    attention_gain_gradient, expert_gain_gradient = (attention_gain, expert_gain)
    dout = group_rows(cotangent.astype(bf16))
    dout_f = dout.astype(f32)
    gate_of_slot = jnp.zeros((experts * CAP,), f32).at[slot].set(gates.reshape(-1))
    slot_grad = (
        jnp.where(filled[:, None] > 0, gate_of_slot[:, None] * dout_f[token_of_slot], 0.0)
        .astype(bf16)
        .reshape(experts, CAP, width)
    )
    gate_grad = jnp.sum(dout_f[:, None, :] * routed, axis=-1)
    owner_g = to_owners(slot_grad, holders)
    owner_hgrad = jnp.dot(owner_g, own_out, preferred_element_type=f32)
    owner_pgrad = jax.vjp(gelu_exact, owner_pre)[1](owner_hgrad)[0].astype(bf16)
    owner_back = jnp.einsum("cf,df->cd", owner_pgrad, own_in, preferred_element_type=f32)
    slot_in_grad = to_groups(owner_back, experts, holders, CAP)
    in_local = jnp.einsum("cd,cf->df", owner_x, owner_pgrad, preferred_element_type=f32)
    out_local = jnp.einsum("cd,cf->df", owner_g, owner_hidden, preferred_element_type=f32)
    in_home, out_home = (
        lax.all_to_all(
            in_local.reshape(width, 1, block_units).astype(jnp.bfloat16),
            "fsdp",
            split_axis=0,
            concat_axis=1,
            tiled=True,
        ).astype(jnp.float32),
        lax.all_to_all(
            out_local.reshape(width, 1, block_units).astype(jnp.bfloat16),
            "fsdp",
            split_axis=0,
            concat_axis=1,
            tiled=True,
        ).astype(jnp.float32),
    )
    in_grad = in_home.reshape(local_rows, experts, units)
    out_grad = out_home.reshape(local_rows, experts, units)
    choice_grad = jnp.sum(picked.astype(f32) * gate_grad[:, :, None], axis=1)
    logit_grad = probs * (choice_grad - jnp.sum(probs * choice_grad, axis=-1, keepdims=True))
    router_part = jnp.einsum("td,te->de", tokens_m.astype(f32), logit_grad, precision=TOP)
    routed_in = slot_in_grad.reshape(experts * CAP, width)[slot].reshape(group, 2, width)
    token_gradient = jnp.sum(routed_in, axis=1) + jnp.einsum(
        "te,de->td", logit_grad, router_back.astype(f32), precision=TOP
    )
    expert_norm_backward, expert_gain_partial, expert_shift_partial = norm_backward(
        owned_rows(token_gradient),
        expert_standardized,
        expert_inverse_deviation,
        expert_gain_gradient,
    )
    middle_grad = cotangent + expert_norm_backward
    mid_rows = group_rows(middle_grad.astype(bf16))
    proj_part = jnp.einsum("th,td->hd", context, mid_rows, preferred_element_type=f32)
    context_grad = jnp.einsum("td,hd->th", mid_rows, proj_back, preferred_element_type=f32).astype(
        bf16
    )
    query_grad, key_grad, value_grad = attend_back(
        proj[0], proj[1], proj[2], lse, context_grad, images
    )
    stacked = jnp.stack([query_grad, key_grad, value_grad])
    qkv_part = jnp.einsum("td,ith->idh", tokens_a, stacked, preferred_element_type=f32)
    attention_input_gradient = owned_rows(
        jnp.einsum("ith,idh->td", stacked, qkv_back, preferred_element_type=f32)
    )
    attention_norm_backward, attention_gain_partial, attention_shift_partial = norm_backward(
        attention_input_gradient,
        attention_standardized,
        attention_inverse_deviation,
        attention_gain_gradient,
    )
    input_grad = middle_grad + attention_norm_backward
    qkv_grad, proj_grad, router_grad, norm_grads = reduce_dense(
        qkv_part,
        proj_part,
        router_part,
        [
            attention_gain_partial,
            attention_shift_partial,
            expert_gain_partial,
            expert_shift_partial,
        ],
    )
    return (
        outputs,
        input_grad,
        norm_grads[0],
        norm_grads[1],
        qkv_grad,
        proj_grad,
        norm_grads[2],
        norm_grads[3],
        router_grad,
        in_grad,
        out_grad,
    )


def solution(mesh):
    return jax.shard_map(
        per_device,
        mesh=mesh,
        in_specs=(
            P(("fsdp", "tp"), None),
            P("fsdp", None),
            P("fsdp"),
            P("fsdp"),
            P(None, "fsdp", "tp"),
            P("tp", "fsdp"),
            P("fsdp"),
            P("fsdp"),
            P("fsdp", None),
            P("fsdp", None, "tp"),
            P("fsdp", None, "tp"),
            P(("fsdp", "tp"), None),
        ),
        out_specs=(
            P(("fsdp", "tp"), None),
            P(("fsdp", "tp"), None),
            P("fsdp"),
            P("fsdp"),
            P(None, "fsdp", "tp"),
            P("tp", "fsdp"),
            P("fsdp"),
            P("fsdp"),
            P("fsdp", None),
            P("fsdp", None, "tp"),
            P("fsdp", None, "tp"),
        ),
        check_vma=False,
    )
```

profile of v0, /device:TPU:0, one launch (start us, length us, event | category | flops | bytes accessed | tf_op | source)
XLA Modules:
  0.0 1606.7 jit_solution(12377187689971864063)
XLA Ops:
  15.1 105.2 %all-gather.3.cloned.1.call-done = bf16[64,12,1556]{2,1,0:T(8,128)(2,1)} async-done(((bf16[1,12,1556]{2,1,0:T(8,128)(2,1)}), bf16[64,12,1556]{2,1,0:T(8,128)(2,1)}) %all-gather.3.cloned.1.call-update) | async-done | bytes 2390032 | tf_op jit(solution)/shard_map/all_gather | solution.py:139
  126.7 11.7 all_gather.16
  201.1 9.7 reduce-scatter.5.cloned.1.call-done
  220.3 19.2 %all_gather.17 = bf16[400,768]{1,0:T(8,128)(2,1)S(1)} all-gather(bf16[200,768]{1,0:T(8,128)(2,1)S(1)} %add_convert_fusion.1), channel_id=1, replica_groups=mesh['fsdp'=64,'tp'=2] {'tp'}, dimensions={0}, use_global_device_ids=true | all-gather | bytes 921600 | tf_op jit(solution)/shard_map/all_gather | solution.py:177
  261.8 60.1 %all_gather.18 = bf16[400,768]{1,0:T(8,128)(2,1)S(1)} all-gather(bf16[200,768]{1,0:T(8,128)(2,1)S(1)} %convert_element_type.180), channel_id=1, replica_groups=mesh['fsdp'=64,'tp'=2] {'tp'}, dimensions={0}, use_global_device_ids=true | all-gather | bytes 921600 | tf_op jit(solution)/shard_map/all_gather | solution.py:177
  345.7 25.8 %all-to-all-start.4 = ((bf16[64,63,768]{2,1,0:T(8,128)(2,1)}), bf16[64,63,768]{2,1,0:T(8,128)(2,1)}, u32[]{:S(2)}, u32[]{:S(2)}) async-start(bf16[64,63,768]{2,1,0:T(8,128)(2,1)} %bitcast.138), calls=%async_computation.6 | async-start | bytes 12582912 | tf_op jit(solution)/shard_map/all_to_all | solution.py:189
  372.8 8.5 reshape.285
  381.3 8.8 fusion.111
  390.1 59.2 %all-to-all-done.4 = bf16[64,63,768]{2,1,0:T(8,128)(2,1)} async-done(((bf16[64,63,768]{2,1,0:T(8,128)(2,1)}), bf16[64,63,768]{2,1,0:T(8,128)(2,1)}, u32[]{:S(2)}, u32[]{:S(2)}) %all-to-all-start.4) | async-done | bytes 6193184 | tf_op jit(solution)/shard_map/all_to_all | solution.py:189
  449.3 8.5 reshape.295
  457.9 20.1 %add_convert_fusion = (bf16[4032,384]{1,0:T(8,128)(2,1)}, f32[4032,384]{1,0:T(8,128)}) fusion(f32[4032,384]{1,0:T(8,128)} %fusion.111, bf16[4032,768]{1,0:T(8,128)(2,1)} %reshape.295, bf16[768,384]{1,0:T(8,128)(2,1)S(1)} %reshape.289), kind=kOutput, calls=%fused_computation.13 | convolution fusion | flops 2489647104 | bytes 22265856 | tf_op jit(solution)/shard_map/dot_general | solution.py:282
  482.6 9.8 fusion.113
  492.4 11.1 all-to-all-start.5
  515.2 9.9 fusion.112
  525.1 143.2 %all-to-all-done.5 = f32[64,63,768]{2,1,0:T(8,128)} async-done(((f32[64,63,768]{2,1,0:T(8,128)}), f32[64,63,768]{2,1,0:T(8,128)}, u32[]{:S(2)}, u32[]{:S(2)}) %all-to-all-start.5) | async-done | bytes 12386336 | tf_op jit(solution)/shard_map/all_to_all | solution.py:196
  668.3 19.0 %all-to-all-start.3 = ((f32[64,63,768]{2,1,0:T(8,128)}), f32[64,63,768]{2,1,0:T(8,128)}, u32[]{:S(2)}, u32[]{:S(2)}) async-start(f32[64,63,768]{2,1,0:T(8,128)} %fusion.112), calls=%async_computation.4 | async-start | bytes 25165824 | tf_op jit(solution)/shard_map/all_to_all | solution.py:196
  713.9 138.2 %all-to-all-done.3 = f32[64,63,768]{2,1,0:T(8,128)} async-done(((f32[64,63,768]{2,1,0:T(8,128)}), f32[64,63,768]{2,1,0:T(8,128)}, u32[]{:S(2)}, u32[]{:S(2)}) %all-to-all-start.3) | async-done | bytes 12386336 | tf_op jit(solution)/shard_map/all_to_all | solution.py:196
  873.7 8.1 multiply_reduce_fusion.1
  889.3 33.0 %reduce-scatter.9.cloned.1.call-done = f32[200,768]{1,0:T(8,128)} async-done(((f32[400,768]{1,0:T(8,128)}), f32[200,768]{1,0:T(8,128)}) %reduce-scatter.9.cloned.1.call-update) | async-done | bytes 614416 | tf_op jit(solution)/shard_map/reduce_scatter | solution.py:181
  923.8 26.5 %reduce-scatter.7.cloned.1.call-done = f32[200,768]{1,0:T(8,128)} async-done(((f32[400,768]{1,0:T(8,128)}), f32[200,768]{1,0:T(8,128)}) %reduce-scatter.7.cloned.1.call-update) | async-done | bytes 614416 | tf_op jit(solution)/shard_map/reduce_scatter | solution.py:181
  952.8 11.2 all_gather.19
  1001.9 13.7 reduce-scatter.11.cloned.1.call-done
  1063.6 9.2 all-to-all-done.7
  1076.9 511.7 %all-reduce.4.cloned.1.call-done = f32[768,1556]{1,0:T(8,128)} async-done(((f32[768,1556]{1,0:T(8,128)}), f32[768,1556]{1,0:T(8,128)}) %all-reduce.4.cloned.1.call-update) | async-done | bytes 4780048
  (254 shorter events, 309.3 us)
Async XLA Ops:
  7.2 113.1 %all-gather.3.cloned.1.call-start = ((), (), s32[]{:S(2)}) async-start(), calls=%async_computation.16 | async-start | bytes 3461120 | tf_op jit(solution)/shard_map/all_gather | solution.py:139
  12.5 198.3 %reduce-scatter.5.cloned.1.call-start = ((), (), s32[]{:S(2)}) async-start(), calls=%async_computation.12 | async-start | bytes 1843200 | tf_op jit(solution)/shard_map/reduce_scatter | solution.py:181
  13.8 151.6 %copy-start.36 = (pred[200]{0:T(512)(128)(4,1)}, pred[200]{0:T(512)(128)(4,1)S(1)}, u32[]{:S(2)}) copy-start(pred[200]{0:T(512)(128)(4,1)S(1)} %iota_compare_fusion.3) | copy-start | bytes 604
  13.8 112.7 %copy-start.27 = (f32[200]{0:T(256)}, f32[200]{0:T(256)S(1)}, u32[]{:S(2)}) copy-start(f32[200]{0:T(256)S(1)} %broadcast_multiply_fusion.6) | copy-start | bytes 2404
  15.1 111.4 %copy-start.31 = (f32[200]{0:T(256)}, f32[200]{0:T(256)S(1)}, u32[]{:S(2)}) copy-start(f32[200]{0:T(256)S(1)} %add_rsqrt_fusion.1) | copy-start | bytes 2404
  124.4 49.6 %copy-start.6 = (bf16[768,1556]{1,0:T(8,128)(2,1)}, bf16[768,1556]{1,0:T(8,128)(2,1)S(1)}, u32[]{:S(2)}) copy-start(bf16[768,1556]{1,0:T(8,128)(2,1)S(1)} %reshape.370) | copy-start | bytes 7170052
  125.0 95.1 %copy-start.24 = (f32[768]{0:T(1024)}, f32[768]{0:T(1024)S(1)}, u32[]{:S(2)}) copy-start(f32[768]{0:T(1024)S(1)} %get-tuple-element.11) | copy-start | bytes 9220
  179.4 32.9 %all-to-all-start.1 = ((bf16[12,64,384]{2,0,1:T(8,128)(2,1)}), bf16[12,64,384]{2,0,1:T(8,128)(2,1)S(1)}, u32[]{:S(2)}, u32[]{:S(2)}) async-start(bf16[12,64,384]{2,0,1:T(8,128)(2,1)} %copy.285), calls=%async_computation.2 | async-start | bytes 1572864 | tf_op jit(solution)/shard_map/all_to_all | solution.py:258
  212.3 37.7 %all-to-all-start.2 = ((bf16[12,64,384]{2,0,1:T(8,128)(2,1)}), bf16[12,64,384]{2,0,1:T(8,128)(2,1)S(1)}, u32[]{:S(2)}, u32[]{:S(2)}) async-start(bf16[12,64,384]{2,0,1:T(8,128)(2,1)} %copy.286), calls=%async_computation.3 | async-start | bytes 1572864 | tf_op jit(solution)/shard_map/all_to_all | solution.py:259
  239.5 91.0 %copy-start = (bf16[400,768]{1,0:T(8,128)(2,1)}, bf16[400,768]{1,0:T(8,128)(2,1)S(1)}, u32[]{:S(2)}) copy-start(bf16[400,768]{1,0:T(8,128)(2,1)S(1)} %all_gather.17) | copy-start | bytes 1843204
  254.8 86.1 %all-to-all-start = ((bf16[64,63,768]{2,1,0:T(8,128)(2,1)}), bf16[64,63,768]{2,1,0:T(8,128)(2,1)}, u32[]{:S(2)}, u32[]{:S(2)}) async-start(bf16[64,63,768]{2,1,0:T(8,128)(2,1)} %bitcast.137), calls=%async_computation.1 | async-start | bytes 12582912 | tf_op jit(solution)/shard_map/all_to_all | solution.py:189
  345.7 103.6 %all-to-all-start.4 = ((bf16[64,63,768]{2,1,0:T(8,128)(2,1)}), bf16[64,63,768]{2,1,0:T(8,128)(2,1)}, u32[]{:S(2)}, u32[]{:S(2)}) async-start(bf16[64,63,768]{2,1,0:T(8,128)(2,1)} %bitcast.138), calls=%async_computation.6 | async-start | bytes 12582912 | tf_op jit(solution)/shard_map/all_to_all | solution.py:189
  492.4 175.9 %all-to-all-start.5 = ((f32[64,63,768]{2,1,0:T(8,128)}), f32[64,63,768]{2,1,0:T(8,128)}, u32[]{:S(2)}, u32[]{:S(2)}) async-start(f32[64,63,768]{2,1,0:T(8,128)} %fusion.113), calls=%async_computation.7 | async-start | bytes 25165824 | tf_op jit(solution)/shard_map/all_to_all | solution.py:196
  668.3 183.8 %all-to-all-start.3 = ((f32[64,63,768]{2,1,0:T(8,128)}), f32[64,63,768]{2,1,0:T(8,128)}, u32[]{:S(2)}, u32[]{:S(2)}) async-start(f32[64,63,768]{2,1,0:T(8,128)} %fusion.112), calls=%async_computation.4 | async-start | bytes 25165824 | tf_op jit(solution)/shard_map/all_to_all | solution.py:196
  687.3 235.0 %reduce-scatter.9.cloned.1.call-start = ((), (), s32[]{:S(2)}) async-start(), calls=%async_computation.14 | async-start | bytes 1843200 | tf_op jit(solution)/shard_map/reduce_scatter | solution.py:181
  885.5 64.8 %reduce-scatter.7.cloned.1.call-start = ((), (), s32[]{:S(2)}) async-start(), calls=%async_computation.13 | async-start | bytes 1843200 | tf_op jit(solution)/shard_map/reduce_scatter | solution.py:181
  886.1 36.3 %copy-start.5 = (f32[200,768]{1,0:T(8,128)S(1)}, f32[200,768]{1,0:T(8,128)}, u32[]{:S(2)}) copy-start(f32[200,768]{1,0:T(8,128)} %copy-done.4) | copy-start | bytes 1843204
  886.1 36.2 %copy-start.25 = (f32[768]{0:T(1024)S(1)}, f32[768]{0:T(1024)}, u32[]{:S(2)}) copy-start(f32[768]{0:T(1024)} %copy-done.24) | copy-start | bytes 9220
  886.1 36.2 %copy-start.30 = (f32[200]{0:T(256)S(1)}, f32[200]{0:T(256)}, u32[]{:S(2)}) copy-start(f32[200]{0:T(256)} %copy-done.29) | copy-start | bytes 2404
  886.1 64.2 %copy-start.9 = (f32[200,768]{1,0:T(8,128)S(1)}, f32[200,768]{1,0:T(8,128)}, u32[]{:S(2)}) copy-start(f32[200,768]{1,0:T(8,128)} %param.23) | copy-start | bytes 1843204
  886.2 129.5 %reduce-scatter.11.cloned.1.call-start = ((), (), s32[]{:S(2)}) async-start(), calls=%async_computation.15 | async-start | bytes 1843200 | tf_op jit(solution)/shard_map/reduce_scatter | solution.py:181
  989.8 598.8 %all-reduce.4.cloned.1.call-start = ((), (), s32[]{:S(2)}) async-start(), calls=%async_computation.17 | async-start | bytes 10223616
  1033.3 21.2 %all-to-all-start.6 = ((bf16[64,2,2304]{2,1,0:T(2,128)(2,1)}), bf16[64,2,2304]{2,1,0:T(2,128)(2,1)S(1)}, u32[]{:S(2)}, u32[]{:S(2)}) async-start(bf16[64,2,2304]{2,1,0:T(2,128)(2,1)} %reshape.401), calls=%async_computation.10 | async-start | bytes 1179648 | tf_op jit(solution)/shard_map/all_to_all | solution.py:289
  1054.5 18.3 %all-to-all-start.7 = ((bf16[64,2,2304]{2,1,0:T(2,128)(2,1)}), bf16[64,2,2304]{2,1,0:T(2,128)(2,1)S(1)}, u32[]{:S(2)}, u32[]{:S(2)}) async-start(bf16[64,2,2304]{2,1,0:T(2,128)(2,1)} %reshape.403), calls=%async_computation.11 | async-start | bytes 1179648 | tf_op jit(solution)/shard_map/all_to_all | solution.py:296
  (28 other events, 338.2 us)
Sparse Core Ops, SparseCore 0:
  12.6 107.5 all-gather.2
  176.7 34.0 reduce-scatter.4
  885.6 36.6 reduce-scatter.8
  924.6 25.6 reduce-scatter.6
  989.9 25.6 reduce-scatter.10
  1023.7 564.9 all-reduce.3
where the time goes:
time: 1620 us; the launch traced here: 1610 us
  waiting for transfers between devices  1050 us (65%)
  local copies, waits for them, and re-layouts  171 us (11%)
  blocking collectives  109 us (7%)
  matrix products  106 us (7%)
  starting transfers between devices  90.5 us (6%)
  other arithmetic  60.1 us (4%)
    unnamed x7, waiting for transfers between devices  512 us
    all_to_all x2, waiting for transfers between devices, to_groups(): lax.all_to_all(pieces, 'fsdp', split_axis=0, concat_axis=0, tiled=True)  281 us
    all_gather x1, waiting for transfers between devices, gather_dense(): full = lax.all_gather(packed, 'fsdp', axis=0, tiled=True)  105 us
    all_gather x4, blocking collectives, group_rows(): return lax.all_gather(value, 'tp', axis=0, tiled=True)  102 us
    reduce_scatter x4, waiting for transfers between devices, owned_rows(): return lax.psum_scatter(value, 'tp', scatter_dimension=0, tiled=True)  83 us
    all_to_all x2, waiting for transfers between devices, to_owners(): lax.all_to_all(spread, 'fsdp', split_axis=0, concat_axis=0, tiled=True)  59.2 us
    all_to_all x2, starting transfers between devices, to_owners(): lax.all_to_all(spread, 'fsdp', split_axis=0, concat_axis=0, tiled=True)  32.8 us
  transfers between devices with their start and end apart: 14, of which 11 were waited for; matrix products, arithmetic and copies ran while one was open for 10% of the time, Pallas kernels for 0%

commit v1 on v0

--- a/solution.py
+++ b/solution.py
@@ -136,7 +136,9 @@
         ],
         axis=1,
     )
-    full = lax.all_gather(packed, "fsdp", axis=0, tiled=True)
+    full = jnp.concatenate(
+        lax.all_to_all(jnp.stack([packed] * lax.axis_size("fsdp")), "fsdp", 0, 0), axis=0
+    )
     width = full.shape[0]
     at = 3 * heads_width
     qkv_full = jnp.transpose(full[:, :at].reshape(width, 3, heads_width), (1, 0, 2))

time: 1620 us -> 1570 us (0.969)
  waiting for transfers between devices: 1050 us -> 992 us
    all_gather x1 -> x0, waiting for transfers between devices: 105 us -> none  [gather_dense(): full = lax.all_gather(packed, 'fsdp', axis=0, tiled=True)]
    all_to_all x0 -> x1, waiting for transfers between devices: none -> 42 us  [gather_dense(): lax.all_to_all(jnp.stack([packed] * lax.axis_size('fsdp')), 'fsdp', 0, 0)]
    unnamed x7 -> x6, waiting for transfers between devices: 512 us -> 512 us
where the time goes in v1:
time: 1570 us; the launch traced here: 1550 us
  waiting for transfers between devices  992 us (63%)
  local copies, waits for them, and re-layouts  172 us (11%)
  blocking collectives  109 us (7%)
  matrix products  106 us (7%)
  starting transfers between devices  101 us (6%)
  other arithmetic  57.9 us (4%)
    unnamed x6, waiting for transfers between devices  512 us
    all_to_all x2, waiting for transfers between devices, to_groups(): lax.all_to_all(pieces, 'fsdp', split_axis=0, concat_axis=0, tiled=True)  281 us
    all_gather x4, blocking collectives, group_rows(): return lax.all_gather(value, 'tp', axis=0, tiled=True)  103 us
    reduce_scatter x4, waiting for transfers between devices, owned_rows(): return lax.psum_scatter(value, 'tp', scatter_dimension=0, tiled=True)  83.6 us
    all_to_all x2, waiting for transfers between devices, to_owners(): lax.all_to_all(spread, 'fsdp', split_axis=0, concat_axis=0, tiled=True)  59.2 us
    all_to_all x1, waiting for transfers between devices, gather_dense(): lax.all_to_all(jnp.stack([packed] * lax.axis_size('fsdp')), 'fsdp', 0, 0)  42 us
    all_to_all x2, starting transfers between devices, to_owners(): lax.all_to_all(spread, 'fsdp', split_axis=0, concat_axis=0, tiled=True)  32.7 us
  transfers between devices with their start and end apart: 14, of which 11 were waited for; matrix products, arithmetic and copies ran while one was open for 10% of the time, Pallas kernels for 0%

profile of v1, /device:TPU:0, one launch (start us, length us, event | category | flops | bytes accessed | tf_op | source)
XLA Modules:
  0.0 1554.4 jit_solution(6359766206836870252)
XLA Ops:
  13.8 9.7 all-to-all-start
  24.1 42.0 %all-to-all-done = bf16[64,12,1556]{2,1,0:T(8,128)(2,1)} async-done(((bf16[64,12,1556]{2,1,0:T(8,128)(2,1)}), bf16[64,12,1556]{2,1,0:T(8,128)(2,1)}, u32[]{:S(2)}, u32[]{:S(2)}) %all-to-all-start) | async-done | bytes 2390048 | tf_op jit(solution)/shard_map/all_to_all | solution.py:140
  72.5 12.4 all_gather.12
  148.2 10.4 reduce-scatter.5.cloned.1.call-done
  168.1 19.2 %all_gather.13 = bf16[400,768]{1,0:T(8,128)(2,1)S(1)} all-gather(bf16[200,768]{1,0:T(8,128)(2,1)S(1)} %add_convert_fusion.1), channel_id=1, replica_groups=mesh['fsdp'=64,'tp'=2] {'tp'}, dimensions={0}, use_global_device_ids=true | all-gather | bytes 921600 | tf_op jit(solution)/shard_map/all_gather | solution.py:179
  209.6 60.1 %all_gather.14 = bf16[400,768]{1,0:T(8,128)(2,1)S(1)} all-gather(bf16[200,768]{1,0:T(8,128)(2,1)S(1)} %convert_element_type.180), channel_id=1, replica_groups=mesh['fsdp'=64,'tp'=2] {'tp'}, dimensions={0}, use_global_device_ids=true | all-gather | bytes 921600 | tf_op jit(solution)/shard_map/all_gather | solution.py:179
  293.5 25.8 %all-to-all-start.5 = ((bf16[64,63,768]{2,1,0:T(8,128)(2,1)}), bf16[64,63,768]{2,1,0:T(8,128)(2,1)}, u32[]{:S(2)}, u32[]{:S(2)}) async-start(bf16[64,63,768]{2,1,0:T(8,128)(2,1)} %bitcast.137), calls=%async_computation.7 | async-start | bytes 12582912 | tf_op jit(solution)/shard_map/all_to_all | solution.py:191
  320.5 8.5 reshape.291
  329.0 8.8 fusion.111
  337.9 59.2 %all-to-all-done.5 = bf16[64,63,768]{2,1,0:T(8,128)(2,1)} async-done(((bf16[64,63,768]{2,1,0:T(8,128)(2,1)}), bf16[64,63,768]{2,1,0:T(8,128)(2,1)}, u32[]{:S(2)}, u32[]{:S(2)}) %all-to-all-start.5) | async-done | bytes 6193184 | tf_op jit(solution)/shard_map/all_to_all | solution.py:191
  397.1 8.5 reshape.301
  405.7 20.1 %add_convert_fusion = (bf16[4032,384]{1,0:T(8,128)(2,1)}, f32[4032,384]{1,0:T(8,128)}) fusion(f32[4032,384]{1,0:T(8,128)} %fusion.111, bf16[4032,768]{1,0:T(8,128)(2,1)} %reshape.301, bf16[768,384]{1,0:T(8,128)(2,1)S(1)} %reshape.295), kind=kOutput, calls=%fused_computation.13 | convolution fusion | flops 2489647104 | bytes 22265856 | tf_op jit(solution)/shard_map/dot_general | solution.py:284
  430.4 9.8 fusion.113
  440.2 11.1 all-to-all-start.6
  462.9 9.9 fusion.112
  472.8 143.2 %all-to-all-done.6 = f32[64,63,768]{2,1,0:T(8,128)} async-done(((f32[64,63,768]{2,1,0:T(8,128)}), f32[64,63,768]{2,1,0:T(8,128)}, u32[]{:S(2)}, u32[]{:S(2)}) %all-to-all-start.6) | async-done | bytes 12386336 | tf_op jit(solution)/shard_map/all_to_all | solution.py:198
  616.1 19.0 %all-to-all-start.4 = ((f32[64,63,768]{2,1,0:T(8,128)}), f32[64,63,768]{2,1,0:T(8,128)}, u32[]{:S(2)}, u32[]{:S(2)}) async-start(f32[64,63,768]{2,1,0:T(8,128)} %fusion.112), calls=%async_computation.5 | async-start | bytes 25165824 | tf_op jit(solution)/shard_map/all_to_all | solution.py:198
  661.6 138.2 %all-to-all-done.4 = f32[64,63,768]{2,1,0:T(8,128)} async-done(((f32[64,63,768]{2,1,0:T(8,128)}), f32[64,63,768]{2,1,0:T(8,128)}, u32[]{:S(2)}, u32[]{:S(2)}) %all-to-all-start.4) | async-done | bytes 12386336 | tf_op jit(solution)/shard_map/all_to_all | solution.py:198
  837.2 32.9 %reduce-scatter.9.cloned.1.call-done = f32[200,768]{1,0:T(8,128)} async-done(((f32[400,768]{1,0:T(8,128)}), f32[200,768]{1,0:T(8,128)}) %reduce-scatter.9.cloned.1.call-update) | async-done | bytes 614416 | tf_op jit(solution)/shard_map/reduce_scatter | solution.py:183
  871.6 26.6 %reduce-scatter.7.cloned.1.call-done = f32[200,768]{1,0:T(8,128)} async-done(((f32[400,768]{1,0:T(8,128)}), f32[200,768]{1,0:T(8,128)}) %reduce-scatter.7.cloned.1.call-update) | async-done | bytes 614416 | tf_op jit(solution)/shard_map/reduce_scatter | solution.py:183
  900.7 11.2 all_gather.15
  949.8 13.8 reduce-scatter.11.cloned.1.call-done
  1011.6 9.2 all-to-all-done.8
  1024.9 511.7 %all-reduce.4.cloned.1.call-done = f32[768,1556]{1,0:T(8,128)} async-done(((f32[768,1556]{1,0:T(8,128)}), f32[768,1556]{1,0:T(8,128)}) %all-reduce.4.cloned.1.call-update) | async-done | bytes 4780048
  (254 shorter events, 317.4 us)
Async XLA Ops:
  13.8 52.2 %all-to-all-start = ((bf16[64,12,1556]{2,1,0:T(8,128)(2,1)}), bf16[64,12,1556]{2,1,0:T(8,128)(2,1)}, u32[]{:S(2)}, u32[]{:S(2)}) async-start(bf16[64,12,1556]{2,1,0:T(8,128)(2,1)} %stack.24), calls=%async_computation | async-start | bytes 6815744 | tf_op jit(solution)/shard_map/all_to_all | solution.py:140
  23.6 135.0 %reduce-scatter.5.cloned.1.call-start = ((), (), s32[]{:S(2)}) async-start(), calls=%async_computation.13 | async-start | bytes 1843200 | tf_op jit(solution)/shard_map/reduce_scatter | solution.py:183
  23.8 88.1 %copy-start.36 = (pred[200]{0:T(512)(128)(4,1)}, pred[200]{0:T(512)(128)(4,1)S(1)}, u32[]{:S(2)}) copy-start(pred[200]{0:T(512)(128)(4,1)S(1)} %iota_compare_fusion.3) | copy-start | bytes 604
  23.8 48.5 %copy-start.27 = (f32[200]{0:T(256)}, f32[200]{0:T(256)S(1)}, u32[]{:S(2)}) copy-start(f32[200]{0:T(256)S(1)} %broadcast_multiply_fusion.6) | copy-start | bytes 2404
  24.0 48.2 %copy-start.31 = (f32[200]{0:T(256)}, f32[200]{0:T(256)S(1)}, u32[]{:S(2)}) copy-start(f32[200]{0:T(256)S(1)} %add_rsqrt_fusion.1) | copy-start | bytes 2404
  70.2 50.2 %copy-start.6 = (bf16[768,1556]{1,0:T(8,128)(2,1)}, bf16[768,1556]{1,0:T(8,128)(2,1)S(1)}, u32[]{:S(2)}) copy-start(bf16[768,1556]{1,0:T(8,128)(2,1)S(1)} %reshape.285) | copy-start | bytes 7170052
  70.8 97.1 %copy-start.24 = (f32[768]{0:T(1024)}, f32[768]{0:T(1024)S(1)}, u32[]{:S(2)}) copy-start(f32[768]{0:T(1024)S(1)} %get-tuple-element.11) | copy-start | bytes 9220
  125.8 34.2 %all-to-all-start.2 = ((bf16[12,64,384]{2,0,1:T(8,128)(2,1)}), bf16[12,64,384]{2,0,1:T(8,128)(2,1)S(1)}, u32[]{:S(2)}, u32[]{:S(2)}) async-start(bf16[12,64,384]{2,0,1:T(8,128)(2,1)} %copy.285), calls=%async_computation.3 | async-start | bytes 1572864 | tf_op jit(solution)/shard_map/all_to_all | solution.py:260
  160.0 37.7 %all-to-all-start.3 = ((bf16[12,64,384]{2,0,1:T(8,128)(2,1)}), bf16[12,64,384]{2,0,1:T(8,128)(2,1)S(1)}, u32[]{:S(2)}, u32[]{:S(2)}) async-start(bf16[12,64,384]{2,0,1:T(8,128)(2,1)} %copy.286), calls=%async_computation.4 | async-start | bytes 1572864 | tf_op jit(solution)/shard_map/all_to_all | solution.py:261
  187.2 91.0 %copy-start = (bf16[400,768]{1,0:T(8,128)(2,1)}, bf16[400,768]{1,0:T(8,128)(2,1)S(1)}, u32[]{:S(2)}) copy-start(bf16[400,768]{1,0:T(8,128)(2,1)S(1)} %all_gather.13) | copy-start | bytes 1843204
  202.6 86.1 %all-to-all-start.1 = ((bf16[64,63,768]{2,1,0:T(8,128)(2,1)}), bf16[64,63,768]{2,1,0:T(8,128)(2,1)}, u32[]{:S(2)}, u32[]{:S(2)}) async-start(bf16[64,63,768]{2,1,0:T(8,128)(2,1)} %bitcast.136), calls=%async_computation.2 | async-start | bytes 12582912 | tf_op jit(solution)/shard_map/all_to_all | solution.py:191
  293.5 103.6 %all-to-all-start.5 = ((bf16[64,63,768]{2,1,0:T(8,128)(2,1)}), bf16[64,63,768]{2,1,0:T(8,128)(2,1)}, u32[]{:S(2)}, u32[]{:S(2)}) async-start(bf16[64,63,768]{2,1,0:T(8,128)(2,1)} %bitcast.137), calls=%async_computation.7 | async-start | bytes 12582912 | tf_op jit(solution)/shard_map/all_to_all | solution.py:191
  440.2 175.9 %all-to-all-start.6 = ((f32[64,63,768]{2,1,0:T(8,128)}), f32[64,63,768]{2,1,0:T(8,128)}, u32[]{:S(2)}, u32[]{:S(2)}) async-start(f32[64,63,768]{2,1,0:T(8,128)} %fusion.113), calls=%async_computation.8 | async-start | bytes 25165824 | tf_op jit(solution)/shard_map/all_to_all | solution.py:198
  616.1 183.8 %all-to-all-start.4 = ((f32[64,63,768]{2,1,0:T(8,128)}), f32[64,63,768]{2,1,0:T(8,128)}, u32[]{:S(2)}, u32[]{:S(2)}) async-start(f32[64,63,768]{2,1,0:T(8,128)} %fusion.112), calls=%async_computation.5 | async-start | bytes 25165824 | tf_op jit(solution)/shard_map/all_to_all | solution.py:198
  635.1 235.0 %reduce-scatter.9.cloned.1.call-start = ((), (), s32[]{:S(2)}) async-start(), calls=%async_computation.15 | async-start | bytes 1843200 | tf_op jit(solution)/shard_map/reduce_scatter | solution.py:183
  833.3 64.9 %reduce-scatter.7.cloned.1.call-start = ((), (), s32[]{:S(2)}) async-start(), calls=%async_computation.14 | async-start | bytes 1843200 | tf_op jit(solution)/shard_map/reduce_scatter | solution.py:183
  834.0 36.1 %copy-start.5 = (f32[200,768]{1,0:T(8,128)S(1)}, f32[200,768]{1,0:T(8,128)}, u32[]{:S(2)}) copy-start(f32[200,768]{1,0:T(8,128)} %copy-done.4) | copy-start | bytes 1843204
  834.0 36.1 %copy-start.25 = (f32[768]{0:T(1024)S(1)}, f32[768]{0:T(1024)}, u32[]{:S(2)}) copy-start(f32[768]{0:T(1024)} %copy-done.24) | copy-start | bytes 9220
  834.1 36.1 %copy-start.30 = (f32[200]{0:T(256)S(1)}, f32[200]{0:T(256)}, u32[]{:S(2)}) copy-start(f32[200]{0:T(256)} %copy-done.29) | copy-start | bytes 2404
  834.1 64.1 %copy-start.9 = (f32[200,768]{1,0:T(8,128)S(1)}, f32[200,768]{1,0:T(8,128)}, u32[]{:S(2)}) copy-start(f32[200,768]{1,0:T(8,128)} %param.23) | copy-start | bytes 1843204
  834.1 129.4 %reduce-scatter.11.cloned.1.call-start = ((), (), s32[]{:S(2)}) async-start(), calls=%async_computation.16 | async-start | bytes 1843200 | tf_op jit(solution)/shard_map/reduce_scatter | solution.py:183
  937.7 598.9 %all-reduce.4.cloned.1.call-start = ((), (), s32[]{:S(2)}) async-start(), calls=%async_computation.17 | async-start | bytes 10223616
  981.2 21.1 %all-to-all-start.7 = ((bf16[64,2,2304]{2,1,0:T(2,128)(2,1)}), bf16[64,2,2304]{2,1,0:T(2,128)(2,1)S(1)}, u32[]{:S(2)}, u32[]{:S(2)}) async-start(bf16[64,2,2304]{2,1,0:T(2,128)(2,1)} %reshape.405), calls=%async_computation.11 | async-start | bytes 1179648 | tf_op jit(solution)/shard_map/all_to_all | solution.py:291
  1002.3 18.4 %all-to-all-start.8 = ((bf16[64,2,2304]{2,1,0:T(2,128)(2,1)}), bf16[64,2,2304]{2,1,0:T(2,128)(2,1)S(1)}, u32[]{:S(2)}, u32[]{:S(2)}) async-start(bf16[64,2,2304]{2,1,0:T(2,128)(2,1)} %reshape.407), calls=%async_computation.12 | async-start | bytes 1179648 | tf_op jit(solution)/shard_map/all_to_all | solution.py:298
  (28 other events, 347.7 us)
Sparse Core Ops, SparseCore 0:
  123.2 35.3 reduce-scatter.4
  833.4 36.6 reduce-scatter.8
  872.5 25.6 reduce-scatter.6
  937.8 25.6 reduce-scatter.10
  971.6 564.9 all-reduce.3
